TPU v7x, 256 devices: a whole 4x4x8 slice. The times are simulated.
256 devices in a mesh: section: 2 (over x_hi), lat: 4 (over x_lo, core), lon: 32 (over y, z).
Axes of the slice: x: 4 (x_hi: 2, x_lo: 2; x = x_hi * 2 + x_lo), y: 4, z: 8, core: 2. Of those that a mesh axis runs over, the one named last changes fastest.
Arguments:
- window_input: bfloat16 [2, 16, 2176, 256], P(None, 'lat', 'lon'), may hold values from -8 to 8
- output_cotangent: bfloat16 [2, 16, 2176, 256], P(None, 'lat', 'lon'), may hold values from -6 to 6
- ocean_mask: int32 [16, 2176], P('lat', 'lon'), may hold values 0 or 1
- dw_kernel: bfloat16 [2, 49, 256], P('section'), may hold values from -1.5 to 1.5
- channel_params: bfloat16 [2, 5, 256], P('section'), may hold values from -1.5 to 1.5
- up_weight: bfloat16 [2, 256, 1024], P('section'), may hold values from -0.375 to 0.375
- up_bias: bfloat16 [2, 1024], P('section'), may hold values from -3 to 3
- down_weight: bfloat16 [2, 1024, 256], P('section'), may hold values from -0.1875 to 0.1875
Outputs:
- boundary: bfloat16 [2, 2, 16, 2176, 256], P('section', None, 'lat', 'lon')
- grad_kernel: float32 [2, 49, 256], P('section')
- grad_channels: float32 [2, 5, 256], P('section')
- grad_up: float32 [2, 256, 1024], P('section')
- grad_up_bias: float32 [2, 1024], P('section')
- grad_down: float32 [2, 1024, 256], P('section')
All inputs are finite; a program needn't handle non-finite values. No bound on the sum of `ocean_mask` on one device may be relied on, other than what follows from the above.
Results may differ from a plain program's by a relative error of at most 0.012.
Values may be sent and summed in bfloat16 or wider, within the bound.
A program may use at most 128 MiB of HBM per device.

v0:
```python
import math
import jax
import jax.numpy as jnp
from jax import lax
from jax.sharding import PartitionSpec as P

KERNEL = 7
ROWS_DEV = 4
COLS_DEV = 68
BATCH = 2
norm_eps = 1e-06
gelu_scale = 0.7978845608028654
gelu_cubic = 0.044715
rows_contract = (((0,), (0,)), ((), ()))
cols_contract = (((1,), (1,)), ((), ()))


def padded_2(block, sides, width, periodic):
    for axis, dim in sides:
        count = lax.axis_size(axis)
        forward = [(i, i + 1) for i in range(count - 1)]
        if periodic:
            forward.append((count - 1, 0))
        backward = [(target, source) for source, target in forward]
        low = lax.ppermute(
            lax.slice_in_dim(block, block.shape[dim] - width, None, axis=dim), axis, forward
        )
        high = lax.ppermute(lax.slice_in_dim(block, 0, width, axis=dim), axis, backward)
        block = jnp.concatenate([low, block, high], axis=dim)
    return block


def from_behind(value, axis, by):
    count = lax.axis_size(axis)
    pairs = [(i, i + by) for i in range(count) if 0 <= i + by < count]
    return lax.ppermute(value, axis, pairs)


def gelu_value(values):
    inner = gelu_scale * (values + gelu_cubic * values * values * values)
    return 0.5 * values * (1.0 + jnp.tanh(inner))


def gelu_slope(values):
    tangent = jnp.tanh(gelu_scale * (values + gelu_cubic * values * values * values))
    return 0.5 * (1.0 + tangent) + 0.5 * values * (1.0 - tangent * tangent) * gelu_scale * (
        1.0 + 3.0 * gelu_cubic * values * values
    )


def depthwise(padded, kernel, row_count, col_count):
    summed = jnp.zeros((padded.shape[0], row_count, col_count, padded.shape[3]), jnp.float32)
    for offset in range(KERNEL * KERNEL):
        row_off, col_off = divmod(offset, KERNEL)
        window = padded[:, row_off : row_off + row_count, col_off : col_off + col_count, :]
        summed = summed + window.astype(jnp.float32) * kernel[offset].astype(jnp.float32)
    return summed


def kernel_grads(padded, grad_conv, row_count, col_count):
    channels = grad_conv.shape[-1]
    grad_wide = grad_conv.astype(jnp.float32)
    tap_sums = []
    for offset in range(KERNEL * KERNEL):
        row_off, col_off = divmod(offset, KERNEL)
        window = padded[:, row_off : row_off + row_count, col_off : col_off + col_count, :].astype(
            jnp.float32
        )
        tap_sums.append(jnp.sum((grad_wide * window).reshape(-1, channels), axis=0))
    return (jnp.stack(tap_sums), jnp.sum(grad_wide.reshape(-1, channels), axis=0))


def cell_forward(conv_out, inputs, sea_mask, params, w_up, b_up, w_down):
    average = jnp.mean(conv_out, axis=-1, keepdims=True)
    centered = conv_out - average
    inverse = lax.rsqrt(jnp.mean(centered * centered, axis=-1, keepdims=True) + norm_eps)
    normed = centered * inverse
    scaled = (normed * params[1].astype(jnp.float32) + params[2].astype(jnp.float32)).astype(
        jnp.bfloat16
    )
    channels = scaled.shape[-1]
    flat_rows = scaled.reshape(-1, channels)
    hidden = jnp.dot(flat_rows, w_up, preferred_element_type=jnp.float32) + b_up.astype(jnp.float32)
    active = gelu_value(hidden).astype(jnp.bfloat16)
    branch = jnp.dot(active, w_down, preferred_element_type=jnp.float32) + params[3].astype(
        jnp.float32
    )
    branch = branch.reshape(conv_out.shape)
    output = (
        sea_mask * (inputs.astype(jnp.float32) + params[4].astype(jnp.float32) * branch)
    ).astype(jnp.bfloat16)
    return (output, (normed, inverse, flat_rows, hidden, active, branch))


def cell_backward(saved, sea_mask, cotangent, params, w_up, w_down):
    normed, inverse, flat_rows, hidden, active, branch = saved
    channels = normed.shape[-1]
    upstream = sea_mask * cotangent.astype(jnp.float32)
    grad_scale = jnp.sum((upstream * branch).reshape(-1, channels), axis=0)
    grad_branch = (
        (params[4].astype(jnp.float32) * upstream).astype(jnp.bfloat16).reshape(-1, channels)
    )
    grad_down = lax.dot_general(
        active, grad_branch, rows_contract, preferred_element_type=jnp.float32
    )
    grad_out_bias = jnp.sum(grad_branch.astype(jnp.float32), axis=0)
    grad_active = lax.dot_general(
        grad_branch, w_down, cols_contract, preferred_element_type=jnp.float32
    )
    grad_hidden = (grad_active * gelu_slope(hidden)).astype(jnp.bfloat16)
    grad_up = lax.dot_general(
        flat_rows, grad_hidden, rows_contract, preferred_element_type=jnp.float32
    )
    grad_up_bias = jnp.sum(grad_hidden.astype(jnp.float32), axis=0)
    grad_scaled = lax.dot_general(
        grad_hidden, w_up, cols_contract, preferred_element_type=jnp.float32
    )
    grad_scaled = grad_scaled.reshape(normed.shape)
    grad_gain = jnp.sum((grad_scaled * normed).reshape(-1, channels), axis=0)
    grad_shift = jnp.sum(grad_scaled.reshape(-1, channels), axis=0)
    grad_normed = grad_scaled * params[1].astype(jnp.float32)
    first_mean = jnp.mean(grad_normed, axis=-1, keepdims=True)
    second_mean = jnp.mean(grad_normed * normed, axis=-1, keepdims=True)
    grad_conv = (inverse * (grad_normed - first_mean - normed * second_mean)).astype(jnp.bfloat16)
    small = (grad_gain, grad_shift, grad_out_bias, grad_scale)
    return (grad_conv, upstream, small, grad_up, grad_up_bias, grad_down)


def halo_field(field):
    reach = KERNEL // 2
    beside_all = padded_2(field, (("lon", 2),), reach, True)
    return padded_2(beside_all, (("lat", 1),), reach, False)


def run_forward(field, sea_mask, weights):
    kernel, params, w_up, b_up, w_down = weights
    padded = halo_field(field)
    conv_out = depthwise(padded, kernel, field.shape[1], field.shape[2]) + params[0].astype(
        jnp.float32
    )
    output, saved = cell_forward(conv_out, field, sea_mask, params, w_up, b_up, w_down)
    return (output, (padded, saved))


def run_backward(stored, sea_mask, weights, cotangent):
    kernel, params, w_up, b_up, w_down = weights
    padded, saved = stored
    row_count, col_count = (cotangent.shape[1], cotangent.shape[2])
    grad_conv, upstream, small, grad_up, grad_bias, grad_down = cell_backward(
        saved, sea_mask, cotangent, params, w_up, w_down
    )
    tap_sums, bias_sum = kernel_grads(padded, grad_conv, row_count, col_count)
    spread = depthwise(halo_field(grad_conv), kernel[::-1], row_count, col_count)
    grad_input = (upstream + spread).astype(jnp.bfloat16)
    return (grad_input, (tap_sums, jnp.stack((bias_sum,) + small), grad_up, grad_bias, grad_down))


def on_device(
    window_input,
    output_cotangent,
    ocean_mask,
    dw_kernel,
    channel_params,
    up_weight,
    up_bias,
    down_weight,
):
    section = lax.axis_index("section")
    first_section = section == 0
    sea_mask = ocean_mask.astype(jnp.float32)[None, :, :, None]
    batch_size = window_input.shape[0]
    local = (dw_kernel[0], channel_params[0], up_weight[0], up_bias[0], down_weight[0])
    micro = 1
    size_micro = batch_size // micro
    zero_field = jnp.zeros((size_micro,) + window_input.shape[1:], jnp.bfloat16)
    received = zero_field
    stored = []
    outputs = []
    for tick in range(micro + 1):
        if tick < micro:
            own_part = window_input
        else:
            own_part = zero_field
        current = jnp.where(first_section, own_part, received)
        result, kept = run_forward(current, sea_mask, local)
        stored.append(kept)
        outputs.append(result)
        if tick < micro:
            received = from_behind(result, "section", 1)
    received = zero_field
    grad_inputs = []
    totals = None
    for tick in range(micro + 1):
        if tick < micro:
            own_part = output_cotangent
        else:
            own_part = zero_field
        current = jnp.where(first_section, received, own_part)
        kept = jax.tree.map(
            lambda before, behind: jnp.where(first_section, before, behind),
            stored[max(tick - 1, 0)],
            stored[min(tick + 1, micro)],
        )
        grad_input, grads = run_backward(kept, sea_mask, local, current)
        counted = jnp.where(
            first_section, 1.0 if tick >= 1 else 0.0, 1.0 if tick < micro else 0.0
        ).astype(jnp.float32)
        weighted = jax.tree.map(lambda member: member * counted, grads)
        if totals is None:
            totals = weighted
        else:
            totals = jax.tree.map(jnp.add, totals, weighted)
        grad_inputs.append(grad_input)
        if tick < micro:
            received = from_behind(grad_input, "section", -1)
    final = jnp.concatenate(outputs[1:], axis=0)
    starts = jnp.concatenate(grad_inputs[1:], axis=0)
    boundary = jnp.where(first_section, starts, final)[None]
    owned = tuple((member[None] for member in totals))
    summed = lax.psum((owned[0], owned[1], owned[2], owned[3], owned[4]), ("lat", "lon"))
    factor = 1.0 / math.sqrt(BATCH * ROWS_DEV * COLS_DEV)
    return (
        boundary,
        summed[0] * factor,
        summed[1] * factor,
        summed[2] * factor,
        summed[3] * factor,
        summed[4] * factor,
    )


def solution(mesh):
    in_specs = (
        P(None, "lat", "lon", None),
        P(None, "lat", "lon", None),
        P("lat", "lon"),
        P("section", None, None),
        P("section", None, None),
        P("section", None, None),
        P("section", None),
        P("section", None, None),
    )
    out_specs = (
        P("section", None, "lat", "lon", None),
        P("section", None, None),
        P("section", None, None),
        P("section", None, None),
        P("section", None),
        P("section", None, None),
    )
    return jax.shard_map(
        on_device, mesh=mesh, in_specs=in_specs, out_specs=out_specs, check_vma=False
    )
```

profile of v0, /device:TPU:4, one launch (start us, length us, event | category | flops | bytes accessed | tf_op | source)
XLA Modules:
  0.0 1807.4 jit_solution(11287534964740938511)
XLA Ops:
  8.4 8.4 collective-permute-start.1
  18.9 4.9 collective-permute-done
  24.0 1.3 collective-permute-start.2
  25.3 1.3 collective-permute-start.3
  28.0 2.1 collective-permute-done.3
  30.9 5.6 fusion.257
  38.1 3.1 fusion.4
  42.2 2.0 convolution_add_fusion.1
  45.4 1.6 multiply_convert_fusion.5
  47.0 1.3 collective-permute-start.4
  48.2 8.8 collective-permute-done.4
  57.6 1.6 collective-permute-start.5
  59.2 1.7 collective-permute-done.6
  60.9 3.7 collective-permute-done.5
  65.6 3.9 collective-permute-start.7
  69.6 1.5 collective-permute-start.8
  71.1 1.7 reshape.2386
  73.1 2.0 collective-permute-done.8
  76.1 5.6 fusion.255
  83.1 4.7 fusion.9
  87.9 1.3 convert_reduce_fusion.3
  91.4 2.2 multiply_reduce_fusion.3
  93.7 1.8 maximum_select_fusion
  95.5 1.7 fusion.145
  98.3 1.8 fusion.146
  100.1 2.0 collective-permute-start.9
  103.8 3.3 collective-permute-done.9
  107.3 5.4 collective-permute-start.11
  112.7 1.5 collective-permute-start.12
  114.2 1.9 convolution_add_fusion
  117.4 4.7 add_convert_fusion.1
  122.2 1.3 collective-permute-start.13
  123.5 1.9 reshape.2391
  127.7 2.0 multiply_reduce_fusion.2
  129.8 2.8 convert_reduce_fusion.2
  132.6 1.9 fusion.254
  135.9 1.7 fusion.219
  138.7 1.9 fusion.220
  143.4 1.7 collective-permute-start.14
  145.1 1.6 fusion.16
  146.8 1.7 fusion.18
  149.3 553.0 %all-reduce = (f32[1,49,256]{2,0,1:T(1,128)S(1)}, f32[1,5,256]{2,0,1:T(1,128)S(1)}, f32[1,1024]{1,0:T(1,128)S(1)}) all-reduce(f32[1,49,256]{2,0,1:T(1,128)S(1)} %multiply_add_fusion.3, f32[1,5,256]{2,0,1:T(1,128)S(1)} %multiply_add_fusion.4, f32[1,1024]{1,0:T(1,128)S(1)} %bitcast.416), channel_id=1, replica_groups=mesh['section'=2,'lat'=4,'lon'=32] {'lat','lon'}, use_global_device_ids=true, to_apply=%region_106.107 | all-reduce | flops 14848 | bytes 118784 | tf_op jit(solution)/shard_map/psum | solution.py:220
  703.4 1.4 collective-permute-start.16
  704.8 1.3 collective-permute-start.17
  707.4 4.9 collective-permute-done.17
  712.8 5.5 fusion.252
  719.1 1078.0 %all-reduce.4.cloned.1.call-done = (f32[1,256,1024]{2,1,0:T(8,128)}, f32[1,1024,256]{2,1,0:T(8,128)}) async-done(((f32[1,256,1024]{2,1,0:T(8,128)}, f32[1,1024,256]{2,1,0:T(8,128)}), (f32[1,256,1024]{2,1,0:T(8,128)}, f32[1,1024,256]{2,1,0:T(8,128)})) %all-reduce.4.cloned.1.call-update) | async-done | bytes 2097168 | tf_op jit(solution)/shard_map/psum | solution.py:220
  1797.0 2.4 broadcast_multiply_fusion.1
  (554 shorter events, 30.5 us)
Async XLA Ops:
  7.2 31.0 %copy-start = (bf16[1,256,1024]{2,1,0:T(8,128)(2,1)S(1)}, bf16[1,256,1024]{2,1,0:T(8,128)(2,1)}, u32[]{:S(2)}) copy-start(bf16[1,256,1024]{2,1,0:T(8,128)(2,1)} %param.13) | copy-start | bytes 1572868
  7.2 1789.8 %all-reduce.4.cloned.1.call-start = ((), (), s32[]{:S(2)}) async-start(), calls=%async_computation | async-start | bytes 4194304 | tf_op jit(solution)/shard_map/psum | solution.py:220
  7.2 19.3 %copy-start.173 = (bf16[1,5,256]{2,1,0:T(8,128)(2,1)S(1)}, bf16[1,5,256]{2,1,0:T(8,128)(2,1)}, u32[]{:S(2)}) copy-start(bf16[1,5,256]{2,1,0:T(8,128)(2,1)} %param.12) | copy-start | bytes 7684
  7.2 19.9 %copy-start.182 = (bf16[1,1024]{1,0:T(2,128)(2,1)S(1)}, bf16[1,1024]{1,0:T(2,128)(2,1)}, u32[]{:S(2)}) copy-start(bf16[1,1024]{1,0:T(2,128)(2,1)} %param.14) | copy-start | bytes 6148
  7.3 20.5 %copy-start.184 = (s32[4,68]{1,0:T(4,128)S(1)}, s32[4,68]{1,0:T(4,128)}, u32[]{:S(2)}) copy-start(s32[4,68]{1,0:T(4,128)} %param.10) | copy-start | bytes 3268
  7.3 20.5 %copy-start.32 = (bf16[1,49,256]{2,1,0:T(8,128)(2,1)S(1)}, bf16[1,49,256]{2,1,0:T(8,128)(2,1)}, u32[]{:S(2)}) copy-start(bf16[1,49,256]{2,1,0:T(8,128)(2,1)} %param.11) | copy-start | bytes 75268
  8.4 10.5 collective-permute-start.1
  16.8 7.1 collective-permute-start
  17.8 13.1 copy-start.39
  17.8 13.1 copy-start.42
  17.8 13.0 copy-start.45
  17.8 13.0 copy-start.48
  17.8 58.0 %copy-start.33 = (f32[1,1,256]{2,1,0:T(1,128)}, f32[1,1,256]{2,1,0:T(1,128)S(1)}, u32[]{:S(2)}) copy-start(f32[1,1,256]{2,1,0:T(1,128)S(1)} %get-tuple-element.177) | copy-start | bytes 3076
  17.8 58.0 %copy-start.35 = (f32[1,1,256]{2,1,0:T(1,128)}, f32[1,1,256]{2,1,0:T(1,128)S(1)}, u32[]{:S(2)}) copy-start(f32[1,1,256]{2,1,0:T(1,128)S(1)} %get-tuple-element.178) | copy-start | bytes 3076
  17.8 58.0 %copy-start.37 = (f32[1,1,256]{2,1,0:T(1,128)}, f32[1,1,256]{2,1,0:T(1,128)S(1)}, u32[]{:S(2)}) copy-start(f32[1,1,256]{2,1,0:T(1,128)S(1)} %get-tuple-element.179) | copy-start | bytes 3076
  18.8 12.1 copy-start.51
  18.8 12.1 copy-start.54
  18.8 12.1 copy-start.58
  18.8 12.1 copy-start.62
  18.8 12.1 copy-start.66
  18.8 12.1 copy-start.70
  18.8 12.1 copy-start.74
  18.8 12.1 copy-start.78
  18.8 12.1 copy-start.82
  18.9 12.1 copy-start.86
  18.9 12.1 copy-start.90
  24.0 4.0 collective-permute-start.2
  25.3 4.8 collective-permute-start.3
  45.3 36.4 %copy-start.4 = (f32[2,4,68,256]{3,2,1,0:T(8,128)}, f32[2,4,68,256]{3,2,1,0:T(8,128)S(1)}, u32[]{:S(2)}) copy-start(f32[2,4,68,256]{3,2,1,0:T(8,128)S(1)} %reshape.2385) | copy-start | bytes 1671172
  47.0 10.1 collective-permute-start.4
  57.1 3.8 collective-permute-start.6
  57.6 7.1 collective-permute-start.5
  65.6 7.5 collective-permute-start.7
  69.6 5.5 collective-permute-start.8
  100.1 14.1 copy-start.25
  100.1 3.7 collective-permute-start.10
  100.1 7.1 collective-permute-start.9
  107.3 9.2 collective-permute-start.11
  112.7 4.0 collective-permute-start.12
  122.2 5.5 collective-permute-start.13
  143.0 559.9 %collective-permute-start.15 = (bf16[2,4,3,256]{3,2,1,0:T(4,128)(2,1)S(1)}, bf16[2,4,3,256]{3,2,1,0:T(4,128)(2,1)S(1)}, u32[]{:S(2)}, u32[]{:S(2)}) collective-permute-start(bf16[2,4,3,256]{3,2,1,0:T(4,128)(2,1)S(1)} %get-tuple-element.158), channel_id=1, source_target_pairs={{1,0},{2,1},{3,2},{4,3},{5,4},{6,5},{7,6},{8,7},{9,8},{10,9},{11,1... | collective-permute-start | bytes 36872 | tf_op jit(solution)/shard_map/ppermute | solution.py:28
  143.4 559.5 %collective-permute-start.14 = (bf16[2,4,3,256]{3,2,1,0:T(4,128)(2,1)S(1)}, bf16[2,4,3,256]{3,2,1,0:T(4,128)(2,1)S(1)}, u32[]{:S(2)}, u32[]{:S(2)}) collective-permute-start(bf16[2,4,3,256]{3,2,1,0:T(4,128)(2,1)S(1)} %get-tuple-element.157), channel_id=1, source_target_pairs={{0,1},{1,2},{2,3},{3,4},{4,5},{5,6},{6,7},{7,8},{8,9},{9,10},{10,1... | collective-permute-start | bytes 36872 | tf_op jit(solution)/shard_map/ppermute | solution.py:25
  703.1 9.4 copy-start.5
  703.1 9.4 copy-start.17
  703.1 9.4 copy-start.57
  703.1 9.4 copy-start.61
  703.4 4.0 collective-permute-start.16
  704.8 7.5 collective-permute-start.17
  (158 other events, 654.4 us)
Sparse Core Ops, SparseCore 0:
  703.0 1093.9 all-reduce.3
where the time goes:
time: 1810 us
  waiting for transfers between devices  1110 us (61%)
  blocking collectives  553 us (31%)
  other arithmetic  51.6 us (3%)
  starting transfers between devices  34.9 us (2%)
  matrix products  23.5 us (1%)
    psum x1, waiting for transfers between devices, on_device(): lax.psum((owned[0], owned[1], owned[2], owned[3], owned[4]), ('lat', 'lon'))  1080 us
    psum x1, blocking collectives, on_device(): lax.psum((owned[0], owned[1], owned[2], owned[3], owned[4]), ('lat', 'lon'))  553 us
  transfers between devices with their start and end apart: 19, of which 12 were waited for; matrix products, arithmetic and copies ran while one was open for 1% of the time, Pallas kernels for 0%

commit v1 on v0

--- a/solution.py
+++ b/solution.py
@@ -3,6 +3,7 @@
 import jax.numpy as jnp
 from jax import lax
 from jax.sharding import PartitionSpec as P
+from jax.lax import psum
 
 KERNEL = 7
 ROWS_DEV = 4
@@ -217,7 +218,7 @@
     starts = jnp.concatenate(grad_inputs[1:], axis=0)
     boundary = jnp.where(first_section, starts, final)[None]
     owned = tuple((member[None] for member in totals))
-    summed = lax.psum((owned[0], owned[1], owned[2], owned[3], owned[4]), ("lat", "lon"))
+    summed = psum(psum((owned[0], owned[1], owned[2], owned[3], owned[4]), "lat"), "lon")
     factor = 1.0 / math.sqrt(BATCH * ROWS_DEV * COLS_DEV)
     return (
         boundary,

time: 1810 us -> 459 us (0.25)
  waiting for transfers between devices: 1110 us -> 169 us
  blocking collectives: 553 us -> 156 us
    psum x1 -> x2, waiting for transfers between devices: 1080 us -> 137 us  [the longest x1 137 us: on_device(): psum(psum((owned[0], owned[1], owned[2], owned[3], owned[4]), 'lat'), 'lon')]
    psum x1 -> x2, blocking collectives: 553 us -> 156 us  [the longest x1 142 us: on_device(): psum(psum((owned[0], owned[1], owned[2], owned[3], owned[4]), 'lat'), 'lon')]
  transfers between devices with their start and end apart: 19 -> 20, of which waited for: 12 -> 12; matrix products, arithmetic and copies ran while one was open for 1% -> 5% of each run, Pallas kernels for 0% -> 0%
where the time goes in v1:
time: 459 us; the launch traced here: 458 us
  waiting for transfers between devices  169 us (37%)
  blocking collectives  156 us (34%)
  other arithmetic  47.8 us (10%)
  starting transfers between devices  35.8 us (8%)
  matrix products  19.6 us (4%)
  between operations  16.5 us (4%)
  local copies, waits for them, and re-layouts  13.8 us (3%)
    psum x1, blocking collectives, on_device(): psum(psum((owned[0], owned[1], owned[2], owned[3], owned[4]), 'lat'), 'lon')  142 us
    psum x1, waiting for transfers between devices, on_device(): psum(psum((owned[0], owned[1], owned[2], owned[3], owned[4]), 'lat'), 'lon')  137 us
    ppermute x8, starting transfers between devices, padded_2(): lax.ppermute(lax.slice_in_dim(block, block.shape[dim] - width, None, axis...  17.9 us
    ppermute x8, starting transfers between devices, padded_2(): lax.ppermute(lax.slice_in_dim(block, 0, width, axis=dim), axis, backward)  14.4 us
    psum x1, blocking collectives, on_device(): psum((owned[0], owned[1], owned[2], owned[3], owned[4]), 'lat')  14.1 us
    ppermute x8, waiting for transfers between devices, padded_2(): lax.ppermute(lax.slice_in_dim(block, block.shape[dim] - width, None, axis...  12 us
    ppermute x8, waiting for transfers between devices, padded_2(): lax.ppermute(lax.slice_in_dim(block, 0, width, axis=dim), axis, backward)  10.5 us
    reduce_sum x2, other arithmetic, cell_forward(): average = jnp.mean(conv_out, axis=-1, keepdims=True)  9.75 us
  transfers between devices with their start and end apart: 20, of which 12 were waited for; matrix products, arithmetic and copies ran while one was open for 5% of the time, Pallas kernels for 0%

profile of v1, /device:TPU:4, one launch (start us, length us, event | category | flops | bytes accessed | tf_op | source)
XLA Modules:
  0.0 458.2 jit_solution(3897846480459124218)
XLA Ops:
  8.4 8.4 %collective-permute-start.1 = (bf16[2,4,3,256]{3,2,1,0:T(4,128)(2,1)S(1)}, bf16[2,4,3,256]{3,2,1,0:T(4,128)(2,1)S(1)}, u32[]{:S(2)}, u32[]{:S(2)}) collective-permute-start(bf16[2,4,3,256]{3,2,1,0:T(4,128)(2,1)S(1)} %get-tuple-element.169), channel_id=1, source_target_pairs={{1,0},{2,1},{3,2},{4,3},{5,4},{6,5},{7,6},{8,7},{9,8},{10,9},{11,1... | collective-permute-start | bytes 36872 | tf_op jit(solution)/shard_map/ppermute | solution.py:29
  18.7 5.1 %collective-permute-done = bf16[2,4,3,256]{3,2,1,0:T(4,128)(2,1)S(1)} collective-permute-done((bf16[2,4,3,256]{3,2,1,0:T(4,128)(2,1)S(1)}, bf16[2,4,3,256]{3,2,1,0:T(4,128)(2,1)S(1)}, u32[]{:S(2)}, u32[]{:S(2)}) %collective-permute-start) | collective-permute-done | bytes 12320 | tf_op jit(solution)/shard_map/ppermute | solution.py:26
  24.0 1.3 collective-permute-start.2
  25.3 1.3 collective-permute-start.3
  28.0 2.1 collective-permute-done.3
  30.8 4.8 %fusion.257 = (f32[2,4,68]{2,1,0:T(4,128)S(1)}, f32[2,4,68,256]{3,2,1,0:T(8,128)S(1)}) fusion(f32[256]{0:T(256)S(1)} %bitcast.424, f32[256]{0:T(256)S(1)} %bitcast.332, bf16[2,7,74,256]{3,2,1,0:T(8,128)(2,1)S(1)} %get-tuple-element.157, f32[256]{0:T(256)S(1)} %bitcast.336, f32[256]{0:T(256)S(1)} %bitcast.224, f32[256]{0:T(256)S(1)} %bitcast.228, ...), kind=kLoop, calls=%fused_computation.622 | loop fusion | flops 23117280 | bytes 12611712 | tf_op jit(solution)/shard_map/reduce_sum | solution.py:75
  36.5 2.3 fusion.4
  41.1 1.3 collective-permute-start.4
  42.4 8.8 %collective-permute-done.4 = bf16[2,4,68,256]{3,2,1,0:T(8,128)(2,1)S(1)} collective-permute-done((bf16[2,4,68,256]{3,2,1,0:T(8,128)(2,1)S(1)}, bf16[2,4,68,256]{3,2,1,0:T(8,128)(2,1)S(1)}, u32[]{:S(2)}, u32[]{:S(2)}) %collective-permute-start.4) | collective-permute-done | bytes 278560 | tf_op jit(solution)/shard_map/ppermute | solution.py:37
  51.6 1.8 collective-permute-start.5
  53.4 1.7 collective-permute-done.6
  55.1 3.6 collective-permute-done.5
  59.5 4.0 collective-permute-start.7
  63.5 1.5 collective-permute-start.8
  66.0 2.8 collective-permute-done.8
  69.7 4.9 %fusion.255 = (f32[2,4,68]{2,1,0:T(4,128)S(1)}, f32[2,4,68,256]{3,2,1,0:T(8,128)S(1)}) fusion(f32[256]{0:T(256)S(1)} %bitcast.425, f32[256]{0:T(256)S(1)} %bitcast.333, bf16[2,7,74,256]{3,2,1,0:T(8,128)(2,1)S(1)} %get-tuple-element.153, f32[256]{0:T(256)S(1)} %bitcast.337, f32[256]{0:T(256)S(1)} %bitcast.225, f32[256]{0:T(256)S(1)} %bitcast.229, ...), kind=kLoop, calls=%fused_computation.621 | loop fusion | flops 23117280 | bytes 12611712 | tf_op jit(solution)/shard_map/reduce_sum | solution.py:75
  75.3 4.7 %fusion.9 = (f32[544,1024]{1,0:T(8,128)S(1)}, bf16[544,1024]{1,0:T(8,128)(2,1)}) fusion(f32[544,1024]{1,0:T(8,128)} %get-tuple-element.229, f32[1024]{0:T(1024)S(1)} %bitcast.533, pred[]{:T(512)S(6)} %eq.3, bf16[544,256]{1,0:T(8,128)(2,1)S(1)} %reshape.2387, bf16[1,256,1024]{2,1,0:T(8,128)(2,1)S(1)} %copy-done), kind=kOutput, calls=%fused_computation.115 | convolution fusion | flops 301367296 | bytes 6377473 | tf_op jit(solution)/shard_map/dot_general | solution.py:84
  80.1 1.3 convert_reduce_fusion.3
  81.4 1.1 fusion.253
  83.4 2.2 multiply_reduce_fusion.3
  85.8 1.9 maximum_select_fusion
  87.6 1.7 fusion.145
  90.4 1.9 fusion.146
  92.3 2.0 collective-permute-start.9
  96.0 3.3 collective-permute-done.9
  99.5 5.4 %collective-permute-start.11 = (bf16[2,3,74,256]{3,2,1,0:T(8,128)(2,1)S(1)}, bf16[2,3,74,256]{3,2,1,0:T(8,128)(2,1)S(1)}, u32[]{:S(2)}, u32[]{:S(2)}) collective-permute-start(bf16[2,3,74,256]{3,2,1,0:T(8,128)(2,1)S(1)} %get-tuple-element.150), channel_id=1, source_target_pairs={{0,32},{32,64},{64,96},{1,33},{33,65},{65,97},{2,34},{34,66},{66,9... | collective-permute-start | bytes 681992 | tf_op jit(solution)/shard_map/ppermute | solution.py:26
  104.9 1.5 collective-permute-start.12
  106.4 1.3 convolution_add_fusion
  109.1 5.4 %add_convert_fusion.1 = bf16[2,4,68,256]{3,2,1,0:T(8,128)(2,1)} fusion(bf16[2,4,68,256]{3,2,1,0:T(8,128)(2,1)S(1)} %get-tuple-element.135, bf16[2,4,3,256]{3,2,1,0:T(4,128)(2,1)S(1)} %collective-permute-done.10, bf16[2,4,3,256]{3,2,1,0:T(4,128)(2,1)S(1)} %collective-permute-done.9, bf16[2,7,74,256]{3,2,1,0:T(8,128)(2,1)S(1)} %get-tuple-element.149, ...), kind=kLoop, calls=%fused_computation.354 | loop fusion | flops 23535616 | bytes 12609601 | tf_op jit(solution)/shard_map/convert_element_type | solution.py:155
  114.5 2.1 collective-permute-start.13
  116.7 1.9 reshape.2391
  120.5 2.7 multiply_reduce_fusion.2
  124.2 2.8 convert_reduce_fusion.2
  127.1 1.1 fusion.254
  128.6 1.7 fusion.219
  131.4 1.3 fusion.220
  135.2 2.0 collective-permute-start.14
  137.3 1.6 fusion.16
  138.8 1.7 fusion.18
  141.6 14.1 %all-reduce.2 = (f32[1,49,256]{2,0,1:T(1,128)S(1)}, f32[1,5,256]{2,0,1:T(1,128)S(1)}, f32[1,1024]{1,0:T(1,128)S(1)}) all-reduce(f32[1,49,256]{2,0,1:T(1,128)S(1)} %multiply_add_fusion.3, f32[1,5,256]{2,0,1:T(1,128)S(1)} %multiply_add_fusion.4, f32[1,1024]{1,0:T(1,128)S(1)} %bitcast.419), channel_id=1, replica_groups=mesh['section'=2,'lat'=4,'lon'=32] {'lat'}, use_global_device_ids=true, to_apply=%region_106.107 | all-reduce | flops 14848 | bytes 118784 | tf_op jit(solution)/shard_map/psum | solution.py:221
  155.7 141.7 %all-reduce = (f32[1,49,256]{2,0,1:T(1,128)S(1)}, f32[1,5,256]{2,0,1:T(1,128)S(1)}, f32[1,1024]{1,0:T(1,128)S(1)}) all-reduce(f32[1,49,256]{2,0,1:T(1,128)S(1)} %get-tuple-element.128, f32[1,5,256]{2,0,1:T(1,128)S(1)} %get-tuple-element.129, ...), channel_id=1, replica_groups=mesh['section'=2,'lat'=4,'lon'=32] {'lon'}, use_global_device_ids=true, to_apply=%region_107.108 | all-reduce | flops 14848 | bytes 118784 | tf_op jit(solution)/shard_map/psum | solution.py:221
  298.5 1.4 collective-permute-start.16
  299.9 1.3 collective-permute-start.17
  302.5 2.4 collective-permute-done.17
  305.2 4.9 %fusion.252 = bf16[1,2,4,68,256]{4,3,2,1,0:T(8,128)(2,1)S(1)} fusion(f32[2,4,68,256]{3,2,1,0:T(8,128)S(1)} %copy-done.9, f32[256]{0:T(256)S(1)} %bitcast.418, f32[4,68]{1,0:T(4,128)S(1)} %convert_element_type.1601, f32[256]{0:T(256)S(1)} %bitcast.223, bf16[2,7,74,256]{3,2,1,0:T(8,128)(2,1)S(1)} %get-tuple-element.145, f32[256]{0:T(256)S(1)} %bitcast.343, ...), kind=kLoop, calls=%fused_computation.427 | loop fusion | flops 24510464 | bytes 13446209 | tf_op jit(solution)/shard_map/broadcast_in_dim | solution.py:219
  311.0 136.9 %all-reduce.7.cloned.1.call-done = (f32[1,256,1024]{2,1,0:T(8,128)}, f32[1,1024,256]{2,1,0:T(8,128)}) async-done(((f32[1,256,1024]{2,1,0:T(8,128)}, f32[1,1024,256]{2,1,0:T(8,128)}), (f32[1,256,1024]{2,1,0:T(8,128)}, f32[1,1024,256]{2,1,0:T(8,128)})) %all-reduce.7.cloned.1.call-update) | async-done | bytes 2097168 | tf_op jit(solution)/shard_map/psum | solution.py:221
  447.8 2.4 broadcast_multiply_fusion.1
  450.3 1.1 broadcast_multiply_fusion
  (472 shorter events, 27.2 us)
Async XLA Ops:
  7.2 29.3 %copy-start = (bf16[1,256,1024]{2,1,0:T(8,128)(2,1)S(1)}, bf16[1,256,1024]{2,1,0:T(8,128)(2,1)}, u32[]{:S(2)}) copy-start(bf16[1,256,1024]{2,1,0:T(8,128)(2,1)} %param.13) | copy-start | bytes 1572868
  7.2 290.9 %all-reduce.9.cloned.1.call-start = ((), (), s32[]{:S(2)}) async-start(), calls=%async_computation.1 | async-start | bytes 4194304 | tf_op jit(solution)/shard_map/psum | solution.py:221
  7.2 19.4 %copy-start.131 = (bf16[1,5,256]{2,1,0:T(8,128)(2,1)S(1)}, bf16[1,5,256]{2,1,0:T(8,128)(2,1)}, u32[]{:S(2)}) copy-start(bf16[1,5,256]{2,1,0:T(8,128)(2,1)} %param.12) | copy-start | bytes 7684
  7.2 19.9 %copy-start.138 = (bf16[1,1024]{1,0:T(2,128)(2,1)S(1)}, bf16[1,1024]{1,0:T(2,128)(2,1)}, u32[]{:S(2)}) copy-start(bf16[1,1024]{1,0:T(2,128)(2,1)} %param.14) | copy-start | bytes 6148
  7.3 20.5 %copy-start.141 = (s32[4,68]{1,0:T(4,128)S(1)}, s32[4,68]{1,0:T(4,128)}, u32[]{:S(2)}) copy-start(s32[4,68]{1,0:T(4,128)} %param.10) | copy-start | bytes 3268
  7.3 20.5 %copy-start.37 = (bf16[1,49,256]{2,1,0:T(8,128)(2,1)S(1)}, bf16[1,49,256]{2,1,0:T(8,128)(2,1)}, u32[]{:S(2)}) copy-start(bf16[1,49,256]{2,1,0:T(8,128)(2,1)} %param.11) | copy-start | bytes 75268
  8.3 22.4 %copy-start.3 = (bf16[2,4,68,256]{3,2,1,0:T(8,128)(2,1)}, bf16[2,4,68,256]{3,2,1,0:T(8,128)(2,1)S(1)}, u32[]{:S(2)}) copy-start(bf16[2,4,68,256]{3,2,1,0:T(8,128)(2,1)S(1)} %copy_select_fusion) | copy-start | bytes 835588
  8.4 10.3 %collective-permute-start.1 = (bf16[2,4,3,256]{3,2,1,0:T(4,128)(2,1)S(1)}, bf16[2,4,3,256]{3,2,1,0:T(4,128)(2,1)S(1)}, u32[]{:S(2)}, u32[]{:S(2)}) collective-permute-start(bf16[2,4,3,256]{3,2,1,0:T(4,128)(2,1)S(1)} %get-tuple-element.169), channel_id=1, source_target_pairs={{1,0},{2,1},{3,2},{4,3},{5,4},{6,5},{7,6},{8,7},{9,8},{10,9},{11,1... | collective-permute-start | bytes 36872 | tf_op jit(solution)/shard_map/ppermute | solution.py:29
  16.8 7.1 %collective-permute-start = (bf16[2,4,3,256]{3,2,1,0:T(4,128)(2,1)S(1)}, bf16[2,4,3,256]{3,2,1,0:T(4,128)(2,1)S(1)}, u32[]{:S(2)}, u32[]{:S(2)}) collective-permute-start(bf16[2,4,3,256]{3,2,1,0:T(4,128)(2,1)S(1)} %get-tuple-element.168), channel_id=1, source_target_pairs={{0,1},{1,2},{2,3},{3,4},{4,5},{5,6},{6,7},{7,8},{8,9},{9,10},{10,1... | collective-permute-start | bytes 36872 | tf_op jit(solution)/shard_map/ppermute | solution.py:26
  18.7 50.7 %copy-start.38 = (f32[1,1,256]{2,1,0:T(1,128)}, f32[1,1,256]{2,1,0:T(1,128)S(1)}, u32[]{:S(2)}) copy-start(f32[1,1,256]{2,1,0:T(1,128)S(1)} %get-tuple-element.217) | copy-start | bytes 3076
  18.7 50.7 %copy-start.41 = (f32[1,1,256]{2,1,0:T(1,128)}, f32[1,1,256]{2,1,0:T(1,128)S(1)}, u32[]{:S(2)}) copy-start(f32[1,1,256]{2,1,0:T(1,128)S(1)} %get-tuple-element.218) | copy-start | bytes 3076
  24.0 4.0 collective-permute-start.2
  25.3 4.8 %collective-permute-start.3 = (bf16[2,3,74,256]{3,2,1,0:T(8,128)(2,1)S(1)}, bf16[2,3,74,256]{3,2,1,0:T(8,128)(2,1)S(1)}, u32[]{:S(2)}, u32[]{:S(2)}) collective-permute-start(bf16[2,3,74,256]{3,2,1,0:T(8,128)(2,1)S(1)} %get-tuple-element.159), channel_id=1, source_target_pairs={{32,0},{64,32},{96,64},{33,1},{65,33},{97,65},{34,2},{66,34},{98,6... | collective-permute-start | bytes 681992 | tf_op jit(solution)/shard_map/ppermute | solution.py:29
  27.2 8.4 %copy-start.128 = (f32[1,1,256]{2,1,0:T(1,128)}, f32[1,1,256]{2,1,0:T(1,128)S(1)}, u32[]{:S(2)}) copy-start(f32[1,1,256]{2,1,0:T(1,128)S(1)} %get-tuple-element.223) | copy-start | bytes 3076
  27.2 9.0 %copy-start.126 = (f32[1,1,256]{2,1,0:T(1,128)}, f32[1,1,256]{2,1,0:T(1,128)S(1)}, u32[]{:S(2)}) copy-start(f32[1,1,256]{2,1,0:T(1,128)S(1)} %get-tuple-element.225) | copy-start | bytes 3076
  27.8 7.8 %copy-start.47 = (f32[1,1,256]{2,1,0:T(1,128)}, f32[1,1,256]{2,1,0:T(1,128)S(1)}, u32[]{:S(2)}) copy-start(f32[1,1,256]{2,1,0:T(1,128)S(1)} %get-tuple-element.190) | copy-start | bytes 3076
  27.8 7.8 %copy-start.51 = (f32[1,1,256]{2,1,0:T(1,128)}, f32[1,1,256]{2,1,0:T(1,128)S(1)}, u32[]{:S(2)}) copy-start(f32[1,1,256]{2,1,0:T(1,128)S(1)} %get-tuple-element.191) | copy-start | bytes 3076
  27.8 7.8 %copy-start.55 = (f32[1,1,256]{2,1,0:T(1,128)}, f32[1,1,256]{2,1,0:T(1,128)S(1)}, u32[]{:S(2)}) copy-start(f32[1,1,256]{2,1,0:T(1,128)S(1)} %get-tuple-element.192) | copy-start | bytes 3076
  27.8 7.8 %copy-start.59 = (f32[1,1,256]{2,1,0:T(1,128)}, f32[1,1,256]{2,1,0:T(1,128)S(1)}, u32[]{:S(2)}) copy-start(f32[1,1,256]{2,1,0:T(1,128)S(1)} %get-tuple-element.193) | copy-start | bytes 3076
  27.8 7.8 %copy-start.63 = (f32[1,1,256]{2,1,0:T(1,128)}, f32[1,1,256]{2,1,0:T(1,128)S(1)}, u32[]{:S(2)}) copy-start(f32[1,1,256]{2,1,0:T(1,128)S(1)} %get-tuple-element.194) | copy-start | bytes 3076
  27.9 7.8 %copy-start.67 = (f32[1,1,256]{2,1,0:T(1,128)}, f32[1,1,256]{2,1,0:T(1,128)S(1)}, u32[]{:S(2)}) copy-start(f32[1,1,256]{2,1,0:T(1,128)S(1)} %get-tuple-element.195) | copy-start | bytes 3076
  27.9 7.8 %copy-start.71 = (f32[1,1,256]{2,1,0:T(1,128)}, f32[1,1,256]{2,1,0:T(1,128)S(1)}, u32[]{:S(2)}) copy-start(f32[1,1,256]{2,1,0:T(1,128)S(1)} %get-tuple-element.196) | copy-start | bytes 3076
  27.9 7.8 %copy-start.75 = (f32[1,1,256]{2,1,0:T(1,128)}, f32[1,1,256]{2,1,0:T(1,128)S(1)}, u32[]{:S(2)}) copy-start(f32[1,1,256]{2,1,0:T(1,128)S(1)} %get-tuple-element.197) | copy-start | bytes 3076
  27.9 7.8 %copy-start.79 = (f32[1,1,256]{2,1,0:T(1,128)}, f32[1,1,256]{2,1,0:T(1,128)S(1)}, u32[]{:S(2)}) copy-start(f32[1,1,256]{2,1,0:T(1,128)S(1)} %get-tuple-element.198) | copy-start | bytes 3076
  27.9 7.8 %copy-start.83 = (f32[1,1,256]{2,1,0:T(1,128)}, f32[1,1,256]{2,1,0:T(1,128)S(1)}, u32[]{:S(2)}) copy-start(f32[1,1,256]{2,1,0:T(1,128)S(1)} %get-tuple-element.199) | copy-start | bytes 3076
  27.9 7.8 %copy-start.87 = (f32[1,1,256]{2,1,0:T(1,128)}, f32[1,1,256]{2,1,0:T(1,128)S(1)}, u32[]{:S(2)}) copy-start(f32[1,1,256]{2,1,0:T(1,128)S(1)} %get-tuple-element.200) | copy-start | bytes 3076
  27.9 7.8 %copy-start.91 = (f32[1,1,256]{2,1,0:T(1,128)}, f32[1,1,256]{2,1,0:T(1,128)S(1)}, u32[]{:S(2)}) copy-start(f32[1,1,256]{2,1,0:T(1,128)S(1)} %get-tuple-element.201) | copy-start | bytes 3076
  27.9 7.8 %copy-start.95 = (f32[1,1,256]{2,1,0:T(1,128)}, f32[1,1,256]{2,1,0:T(1,128)S(1)}, u32[]{:S(2)}) copy-start(f32[1,1,256]{2,1,0:T(1,128)S(1)} %get-tuple-element.202) | copy-start | bytes 3076
  28.0 41.5 %copy-start.44 = (f32[1,1,256]{2,1,0:T(1,128)}, f32[1,1,256]{2,1,0:T(1,128)S(1)}, u32[]{:S(2)}) copy-start(f32[1,1,256]{2,1,0:T(1,128)S(1)} %get-tuple-element.189) | copy-start | bytes 3076
  41.1 10.1 %collective-permute-start.4 = (bf16[2,4,68,256]{3,2,1,0:T(8,128)(2,1)S(1)}, bf16[2,4,68,256]{3,2,1,0:T(8,128)(2,1)S(1)}, u32[]{:S(2)}, u32[]{:S(2)}) collective-permute-start(bf16[2,4,68,256]{3,2,1,0:T(8,128)(2,1)S(1)} %get-tuple-element.227), channel_id=1, source_target_pairs={{0,128},{1,129},{2,130},{3,131},{4,132},{5,133},{6,134},{7,135},{8... | collective-permute-start | bytes 835592 | tf_op jit(solution)/shard_map/ppermute | solution.py:37
  51.2 8.3 %copy-start.21 = (bf16[2,4,68,256]{3,2,1,0:T(8,128)(2,1)}, bf16[2,4,68,256]{3,2,1,0:T(8,128)(2,1)S(1)}, u32[]{:S(2)}) copy-start(bf16[2,4,68,256]{3,2,1,0:T(8,128)(2,1)S(1)} %collective-permute-done.4) | copy-start | bytes 835588
  51.2 23.4 %copy-start.5 = (bf16[2,4,68,256]{3,2,1,0:T(8,128)(2,1)}, bf16[2,4,68,256]{3,2,1,0:T(8,128)(2,1)S(1)}, u32[]{:S(2)}) copy-start(bf16[2,4,68,256]{3,2,1,0:T(8,128)(2,1)S(1)} %broadcast_select_fusion.5) | copy-start | bytes 835588
  51.3 3.8 collective-permute-start.6
  51.6 7.1 %collective-permute-start.5 = (bf16[2,4,3,256]{3,2,1,0:T(4,128)(2,1)S(1)}, bf16[2,4,3,256]{3,2,1,0:T(4,128)(2,1)S(1)}, u32[]{:S(2)}, u32[]{:S(2)}) collective-permute-start(bf16[2,4,3,256]{3,2,1,0:T(4,128)(2,1)S(1)} %get-tuple-element.166), channel_id=1, source_target_pairs={{0,1},{1,2},{2,3},{3,4},{4,5},{5,6},{6,7},{7,8},{8,9},{9,10},{10,1... | collective-permute-start | bytes 36872 | tf_op jit(solution)/shard_map/ppermute | solution.py:26
  59.5 6.5 %collective-permute-start.7 = (bf16[2,3,74,256]{3,2,1,0:T(8,128)(2,1)}, bf16[2,3,74,256]{3,2,1,0:T(8,128)(2,1)S(1)}, u32[]{:S(2)}, u32[]{:S(2)}) collective-permute-start(bf16[2,3,74,256]{3,2,1,0:T(8,128)(2,1)} %get-tuple-element.154), channel_id=1, source_target_pairs={{0,32},{32,64},{64,96},{1,33},{33,65},{65,97},{2,34},{34,66},{66,9... | collective-permute-start | bytes 681992 | tf_op jit(solution)/shard_map/ppermute | solution.py:26
  63.5 5.2 %collective-permute-start.8 = (bf16[2,3,74,256]{3,2,1,0:T(8,128)(2,1)S(1)}, bf16[2,3,74,256]{3,2,1,0:T(8,128)(2,1)S(1)}, u32[]{:S(2)}, u32[]{:S(2)}) collective-permute-start(bf16[2,3,74,256]{3,2,1,0:T(8,128)(2,1)S(1)} %get-tuple-element.155), channel_id=1, source_target_pairs={{32,0},{64,32},{96,64},{33,1},{65,33},{97,65},{34,2},{66,34},{98,6... | collective-permute-start | bytes 681992 | tf_op jit(solution)/shard_map/ppermute | solution.py:29
  92.3 14.1 %copy-start.30 = (bf16[544,1024]{1,0:T(8,128)(2,1)S(1)}, bf16[544,1024]{1,0:T(8,128)(2,1)}, u32[]{:S(2)}) copy-start(bf16[544,1024]{1,0:T(8,128)(2,1)} %get-tuple-element.143) | copy-start | bytes 3342340
  92.3 14.1 %copy-start.125 = (f32[1,1,256]{2,1,0:T(1,128)S(1)}, f32[1,1,256]{2,1,0:T(1,128)}, u32[]{:S(2)}) copy-start(f32[1,1,256]{2,1,0:T(1,128)} %get-tuple-element.224) | copy-start | bytes 3076
  92.3 3.7 collective-permute-start.10
  92.3 7.1 %collective-permute-start.9 = (bf16[2,4,3,256]{3,2,1,0:T(4,128)(2,1)S(1)}, bf16[2,4,3,256]{3,2,1,0:T(4,128)(2,1)S(1)}, u32[]{:S(2)}, u32[]{:S(2)}) collective-permute-start(bf16[2,4,3,256]{3,2,1,0:T(4,128)(2,1)S(1)} %get-tuple-element.164), channel_id=1, source_target_pairs={{0,1},{1,2},{2,3},{3,4},{4,5},{5,6},{6,7},{7,8},{8,9},{9,10},{10,1... | collective-permute-start | bytes 36872 | tf_op jit(solution)/shard_map/ppermute | solution.py:26
  99.5 8.4 %collective-permute-start.11 = (bf16[2,3,74,256]{3,2,1,0:T(8,128)(2,1)S(1)}, bf16[2,3,74,256]{3,2,1,0:T(8,128)(2,1)S(1)}, u32[]{:S(2)}, u32[]{:S(2)}) collective-permute-start(bf16[2,3,74,256]{3,2,1,0:T(8,128)(2,1)S(1)} %get-tuple-element.150), channel_id=1, source_target_pairs={{0,32},{32,64},{64,96},{1,33},{33,65},{65,97},{2,34},{34,66},{66,9... | collective-permute-start | bytes 681992 | tf_op jit(solution)/shard_map/ppermute | solution.py:26
  104.9 3.9 collective-permute-start.12
  114.5 6.0 %collective-permute-start.13 = (bf16[2,4,68,256]{3,2,1,0:T(8,128)(2,1)}, bf16[2,4,68,256]{3,2,1,0:T(8,128)(2,1)}, u32[]{:S(2)}, u32[]{:S(2)}) collective-permute-start(bf16[2,4,68,256]{3,2,1,0:T(8,128)(2,1)} %add_convert_fusion.1), channel_id=1, source_target_pairs={{128,0},{129,1},{130,2},{131,3},{132,4},{133,5},{134,6},{135,7},{1... | collective-permute-start | bytes 835592 | tf_op jit(solution)/shard_map/ppermute | solution.py:37
  135.1 162.9 %collective-permute-start.15 = (bf16[2,4,3,256]{3,2,1,0:T(4,128)(2,1)S(1)}, bf16[2,4,3,256]{3,2,1,0:T(4,128)(2,1)S(1)}, u32[]{:S(2)}, u32[]{:S(2)}) collective-permute-start(bf16[2,4,3,256]{3,2,1,0:T(4,128)(2,1)S(1)} %get-tuple-element.163), channel_id=1, source_target_pairs={{1,0},{2,1},{3,2},{4,3},{5,4},{6,5},{7,6},{8,7},{9,8},{10,9},{11,1... | collective-permute-start | bytes 36872 | tf_op jit(solution)/shard_map/ppermute | solution.py:29
  135.2 162.8 %collective-permute-start.14 = (bf16[2,4,3,256]{3,2,1,0:T(4,128)(2,1)S(1)}, bf16[2,4,3,256]{3,2,1,0:T(4,128)(2,1)S(1)}, u32[]{:S(2)}, u32[]{:S(2)}) collective-permute-start(bf16[2,4,3,256]{3,2,1,0:T(4,128)(2,1)S(1)} %get-tuple-element.162), channel_id=1, source_target_pairs={{0,1},{1,2},{2,3},{3,4},{4,5},{5,6},{6,7},{7,8},{8,9},{9,10},{10,1... | collective-permute-start | bytes 36872 | tf_op jit(solution)/shard_map/ppermute | solution.py:26
  141.1 306.7 %all-reduce.7.cloned.1.call-start = ((), (), s32[]{:S(2)}) async-start(), calls=%async_computation | async-start | bytes 4194304 | tf_op jit(solution)/shard_map/psum | solution.py:221
  298.5 4.0 collective-permute-start.16
  299.9 4.9 %collective-permute-start.17 = (bf16[2,3,74,256]{3,2,1,0:T(8,128)(2,1)S(1)}, bf16[2,3,74,256]{3,2,1,0:T(8,128)(2,1)S(1)}, u32[]{:S(2)}, u32[]{:S(2)}) collective-permute-start(bf16[2,3,74,256]{3,2,1,0:T(8,128)(2,1)S(1)} %get-tuple-element.147), channel_id=1, source_target_pairs={{32,0},{64,32},{96,64},{33,1},{65,33},{97,65},{34,2},{66,34},{98,6... | collective-permute-start | bytes 681992 | tf_op jit(solution)/shard_map/ppermute | solution.py:29
  (116 other events, 409.4 us)
Sparse Core Ops, SparseCore 0:
  141.2 63.1 all-reduce.8
  298.2 149.6 all-reduce.6
